TPU v7x, 512 devices: a whole 4x4x16 slice. The times are simulated.
512 devices in a mesh: group: 4 (over y), lat: 16 (over z_hi, x), lon: 8 (over z_lo, core).
Axes of the slice: x: 4, y: 4, z: 16 (z_hi: 4, z_lo: 4; z = z_hi * 4 + z_lo), core: 2. Of those that a mesh axis runs over, the one named last changes fastest.
Arguments:
- species_amounts: float32 [128, 4, 256, 1024], P('group', None, 'lat', 'lon'), may hold values from -4 to 4
- zonal_cell_fraction: float32 [4, 256, 1024], P('group', 'lat', 'lon'), may hold values from -0.3 to 0.3
- meridional_cell_fraction: float32 [4, 256, 1024], P('group', 'lat', 'lon'), may hold values from -0.3 to 0.3
- updraft_cell_fraction: float32 [4, 256, 1024], P('group', 'lat', 'lon'), may hold values from -0.3 to 0.3
- warmth_anomaly: float32 [4, 256, 1024], P('group', 'lat', 'lon'), may hold values from -2 to 2
- mass_per_volume: float32 [4, 256, 1024], P('group', 'lat', 'lon'), may hold values from 0.5 to 2
- chemistry_iterations: int32 [256, 1024], P('lat', 'lon'), may hold values from 1 to 2, as said below
- companion_species: bfloat16 [512, 128], replicated, may hold values from -0.5 to 0.5
- stoichiometric_rate: bfloat16 [128, 512], replicated, may hold values from -0.25 to 0.25
- heat_yield: float32 [128], replicated, may hold values from -0.5 to 0.5
Outputs:
- tracers_out: float32 [128, 4, 256, 1024], P('group', None, 'lat', 'lon')
- east_out: float32 [4, 256, 1024], P('group', 'lat', 'lon')
- north_out: float32 [4, 256, 1024], P('group', 'lat', 'lon')
- temp_out: float32 [4, 256, 1024], P('group', 'lat', 'lon')
Inputs may be any that keep to these rules, and one draw needn't show every extreme that they name: `chemistry_iterations`: columns at latitude rows 192 and above hold 1 or 2, and the last row holds 2; all other columns hold 1.
All inputs are finite; a program needn't handle non-finite values.
Results may differ from a plain program's by a relative error of at most 0.0011.
Values sent between devices are 32-bit elements; how exact they have to be, the bound alone decides.
A program may use at most 64 MiB of HBM per device.

v0:
```python
import jax
import jax.numpy as jnp
from jax import lax
from jax.sharding import PartitionSpec as P

diffusion = 0.1
pressure = 0.05
chem_step = 0.2
block_cells = 512


def cut_along(value, dim, devices):
    lengths = value.shape
    pieces = value.reshape(*lengths[:dim], devices, lengths[dim] // devices, *lengths[dim + 1 :])
    return jnp.moveaxis(pieces, dim, 0)


def joined_along(pieces, dim):
    lengths = list(pieces.shape[1:])
    lengths[dim] *= pieces.shape[0]
    return jnp.moveaxis(pieces, 0, dim).reshape(lengths)


def one_exchange(value, axis, axes, splits, concats):
    sizes = [lax.axis_size(a) for a in axes]
    pieces = cut_along(value, splits[0], sizes[0])
    pieces = jnp.moveaxis(cut_along(pieces, splits[1] + 1, sizes[1]), 0, 1)
    inside = pieces.shape[2:]
    pieces = pieces.reshape(-1, *inside)
    pieces = lax.all_to_all(pieces, axis, split_axis=0, concat_axis=0, tiled=True)
    pieces = joined_along(pieces.reshape(*sizes, *inside), concats[0] + 1)
    return joined_along(pieces, concats[1])


def extended(value, sides, width):
    edges = {}
    for axis, dim in sides:
        devices, length = (lax.axis_size(axis), value.shape[dim])
        up = [(i, (i + 1) % devices) for i in range(devices - 1)]
        last = lax.slice_in_dim(value, length - width, length, axis=dim)
        leading = lax.slice_in_dim(value, 0, width, axis=dim)
        edges[dim] = (
            lax.ppermute(last, axis, up),
            lax.ppermute(leading, axis, [(b, a) for a, b in up]),
        )
    done = []
    for _, dim in sides:
        low, high = edges[dim]
        around = [(width, width) if d in done else (0, 0) for d in range(value.ndim)]
        value = jnp.concatenate([jnp.pad(low, around), value, jnp.pad(high, around)], axis=dim)
        done.append(dim)
    return value


def transport(padded, east_pad, north_pad, upward):
    zonal_cells = padded[..., 1:-1, :]
    zonal_wind = east_pad[:, 1:-1, :]
    face_wind = 0.5 * (zonal_wind[..., :-1] + zonal_wind[..., 1:])
    face_flux = (
        jnp.maximum(face_wind, 0.0) * zonal_cells[..., :-1]
        + jnp.minimum(face_wind, 0.0) * zonal_cells[..., 1:]
    )
    change = face_flux[..., 1:] - face_flux[..., :-1]
    north_cells = padded[..., 1:-1]
    north_wind = north_pad[:, :, 1:-1]
    face_wind = 0.5 * (north_wind[:, :-1] + north_wind[:, 1:])
    face_flux = (
        jnp.maximum(face_wind, 0.0) * north_cells[..., :-1, :]
        + jnp.minimum(face_wind, 0.0) * north_cells[..., 1:, :]
    )
    change = change + (face_flux[..., 1:, :] - face_flux[..., :-1, :])
    centre = padded[..., 1:-1, 1:-1]
    face_wind = 0.5 * (upward[:-1] + upward[1:])
    face_flux = (
        jnp.maximum(face_wind, 0.0) * centre[..., :-1, :, :]
        + jnp.minimum(face_wind, 0.0) * centre[..., 1:, :, :]
    )
    closed = jnp.zeros_like(face_flux[..., :1, :, :])
    face_flux = jnp.concatenate([closed, face_flux, closed], axis=-3)
    change = change + (face_flux[..., 1:, :, :] - face_flux[..., :-1, :, :])
    return centre - change


def dynamics(padded):
    centre = padded[:, :, 1:-1, 1:-1]
    eastern = padded[:, :, 1:-1, 2:]
    western = padded[:, :, 1:-1, :-2]
    northern = padded[:, :, 2:, 1:-1]
    southern = padded[:, :, :-2, 1:-1]
    laplace = eastern + western + northern + southern - 4.0 * centre
    diffused = centre + diffusion * laplace
    zonal_axis_name = diffused[0] - pressure * (eastern[2] - western[2])
    meridional_axis_name = diffused[1] - pressure * (northern[2] - southern[2])
    return (zonal_axis_name, meridional_axis_name, diffused[2])


def react_block(
    tracer_block, rate_block, count_block, companion_species, stoichiometric_rate, heat_yield
):
    species = tracer_block.shape[0]
    width = tracer_block.shape[1]
    repeats = companion_species.shape[0] // species
    deepest = jnp.max(count_block)

    def keep_going(state_pair):
        return state_pair[0] < deepest

    def substep(state_pair):
        counter, current = state_pair
        narrow = current.astype(jnp.bfloat16)
        pair_terms = jnp.dot(companion_species, narrow, preferred_element_type=jnp.float32)
        quadratic = (
            (pair_terms.reshape(repeats, species, width) * current[None])
            .reshape(repeats * species, width)
            .astype(jnp.bfloat16)
        )
        tendency = (
            rate_block[None]
            * jnp.dot(stoichiometric_rate, quadratic, preferred_element_type=jnp.float32)
            - current
        )
        current = jnp.where(counter < count_block[None], current + chem_step * tendency, current)
        return (counter + 1, current)

    final = lax.while_loop(keep_going, substep, (jnp.zeros((), jnp.int32), tracer_block))[1]
    heating = jnp.dot(heat_yield[None], final - tracer_block, precision=lax.Precision.HIGHEST)[0]
    return (final, heating)


def react_cells(
    tracer_cells, rate_cells, count_cells, companion_species, stoichiometric_rate, heat_yield
):
    cell_count = tracer_cells.shape[1]
    sort_order = jnp.argsort(-count_cells, stable=True)
    inverse = jnp.argsort(sort_order)
    sorted_tracers = jnp.take(tracer_cells, sort_order, axis=1)
    sorted_rates = jnp.take(rate_cells, sort_order)
    sorted_counts = jnp.take(count_cells, sort_order)

    def one_block(block_index, outputs):
        offset = block_index * block_cells
        tracer_block = lax.dynamic_slice_in_dim(sorted_tracers, offset, block_cells, 1)
        rate_block = lax.dynamic_slice_in_dim(sorted_rates, offset, block_cells, 0)
        count_block = lax.dynamic_slice_in_dim(sorted_counts, offset, block_cells, 0)
        final, heating = react_block(
            tracer_block,
            rate_block,
            count_block,
            companion_species,
            stoichiometric_rate,
            heat_yield,
        )
        return (
            lax.dynamic_update_slice_in_dim(outputs[0], final, offset, 1),
            lax.dynamic_update_slice_in_dim(outputs[1], heating, offset, 0),
        )

    reacted, heated = lax.fori_loop(
        0,
        cell_count // block_cells,
        one_block,
        (jnp.zeros_like(sorted_tracers), jnp.zeros_like(sorted_rates)),
    )
    return (jnp.take(reacted, inverse, axis=1), jnp.take(heated, inverse))


def scattered(
    advected,
    reaction_rate,
    chemistry_iterations,
    companion_species,
    stoichiometric_rate,
    heat_yield,
):
    groups = lax.axis_size("group")
    own_group = lax.axis_index("group")
    stratum_total = advected.shape[1]
    meridian_span = advected.shape[2]
    parallel_span = advected.shape[3]
    column_part = parallel_span // groups
    count_field = jnp.broadcast_to(
        chemistry_iterations.astype(jnp.float32)[None],
        (stratum_total, meridian_span, parallel_span),
    )
    own_rates = lax.dynamic_slice_in_dim(reaction_rate, own_group * column_part, column_part, 2)
    own_counts = lax.dynamic_slice_in_dim(count_field, own_group * column_part, column_part, 2)
    cell_info = jnp.concatenate([own_rates, own_counts], axis=2)[None, :, None]
    arrived, info_in = (
        one_exchange(advected[:, :, None], ("group", "lat"), ("group", "lat"), (1, 3), (0, 2)),
        one_exchange(cell_info, ("group", "lat"), ("group", "lat"), (1, 3), (0, 2)),
    )
    species = arrived.shape[0]
    cell_shape = arrived.shape[1:]
    cell_data = info_in.reshape(groups, cell_shape[0], cell_shape[1], cell_shape[2], 2, column_part)
    cell_data = cell_data.transpose(4, 1, 2, 3, 0, 5).reshape(2, -1)
    reacted, heating = react_cells(
        arrived.reshape(species, -1),
        cell_data[0],
        cell_data[1].astype(jnp.int32),
        companion_species,
        stoichiometric_rate,
        heat_yield,
    )
    heat_copies = jnp.broadcast_to(heating.reshape((1,) + cell_shape), (groups,) + cell_shape)
    returned, heat_back = (
        one_exchange(
            reacted.reshape(arrived.shape), ("group", "lat"), ("group", "lat"), (0, 2), (1, 3)
        ),
        one_exchange(heat_copies, ("group", "lat"), ("group", "lat"), (0, 2), (1, 3)),
    )
    return (returned[:, :, 0], heat_back[0, :, 0])


def local(
    species_amounts,
    zonal_cell_fraction,
    meridional_cell_fraction,
    updraft_cell_fraction,
    warmth_anomaly,
    mass_per_volume,
    chemistry_iterations,
    companion_species,
    stoichiometric_rate,
    heat_yield,
):
    own_group = lax.axis_index("group")
    local_strata = warmth_anomaly.shape[0]
    owned_tracers = species_amounts.shape[0]
    columns = lax.all_gather(
        jnp.stack(
            [
                zonal_cell_fraction,
                meridional_cell_fraction,
                updraft_cell_fraction,
                warmth_anomaly,
                mass_per_volume,
            ]
        ),
        "group",
        axis=1,
        tiled=True,
    )
    zonal_axis_name, meridional_axis_name, upward, heat_snapshot, air_density = (
        columns[0],
        columns[1],
        columns[2],
        columns[3],
        columns[4],
    )
    stacked = jnp.concatenate(
        [species_amounts, jnp.stack([zonal_axis_name, meridional_axis_name, heat_snapshot])], axis=0
    )
    padded = extended(stacked, (("lat", 2), ("lon", 3)), 1)
    advected = transport(
        padded[:owned_tracers], padded[owned_tracers], padded[owned_tracers + 1], upward
    )
    new_east, new_north, warmed = dynamics(padded[owned_tracers:])
    reaction_rate = jax.nn.sigmoid(2.0 * heat_snapshot)
    reacted, heating = scattered(
        advected,
        reaction_rate,
        chemistry_iterations,
        companion_species,
        stoichiometric_rate,
        heat_yield,
    )
    heat_snapshot = warmed + heating / air_density
    start_level = own_group * local_strata
    east_mine = lax.dynamic_slice_in_dim(new_east, start_level, local_strata, 0)
    north_mine = lax.dynamic_slice_in_dim(new_north, start_level, local_strata, 0)
    thermal_mine = lax.dynamic_slice_in_dim(heat_snapshot, start_level, local_strata, 0)
    return (reacted, east_mine, north_mine, thermal_mine)


def solution(mesh):
    return jax.shard_map(
        local,
        mesh=mesh,
        in_specs=(
            P("group", None, "lat", "lon"),
            P("group", "lat", "lon"),
            P("group", "lat", "lon"),
            P("group", "lat", "lon"),
            P("group", "lat", "lon"),
            P("group", "lat", "lon"),
            P("lat", "lon"),
            P(),
            P(),
            P(),
        ),
        out_specs=(
            P("group", None, "lat", "lon"),
            P("group", "lat", "lon"),
            P("group", "lat", "lon"),
            P("group", "lat", "lon"),
        ),
        check_vma=False,
    )
```

profile of v0, /device:TPU:2, one launch (start us, length us, event | category | flops | bytes accessed | tf_op | source)
XLA Modules:
  0.0 286.0 jit_solution(10840602657939708706)
XLA Ops:
  0.6 0.8 constant_dynamic-update-slice_fusion.5
  4.2 12.6 %all_gather.3 = f32[5,4,16,128]{3,2,1,0:T(8,128)S(1)} all-gather(f32[5,1,16,128]{3,2,1,0:T(8,128)S(1)} %constant_dynamic-update-slice_fusion.1), channel_id=1, replica_groups=mesh['group'=4,'lat'=16,'lon'=8] {'group'}, dimensions={1}, use_global_device_ids=true | all-gather | bytes 204800 | tf_op jit(solution)/shard_map/all_gather | solution.py:229
  17.4 0.8 dynamic-slice_convert_fusion
  19.0 20.6 %all-to-all-start.1 = ((f32[64,1,1,1,1,64]{5,4,3,2,1,0:T(1,128)}), f32[64,1,1,1,1,64]{5,4,3,2,1,0:T(1,128)S(1)}, u32[]{:S(2)}, u32[]{:S(2)}) async-start(f32[64,1,1,1,1,64]{5,4,3,2,1,0:T(1,128)} %bitcast.11), calls=%async_computation.1 | async-start | bytes 65536 | tf_op jit(solution)/shard_map/all_to_all | solution.py:30
  39.6 2.0 pad_maximum_fusion.11
  41.6 3.4 %collective-permute-start.1 = (f32[35,4,1,128]{3,2,1,0:T(1,128)}, f32[35,4,1,128]{3,2,1,0:T(1,128)S(1)}, u32[]{:S(2)}, u32[]{:S(2)}) collective-permute-start(f32[35,4,1,128]{3,2,1,0:T(1,128)} %get-tuple-element.257), channel_id=1, source_target_pairs={{0,8},{8,16},{16,24},{24,32},{32,40},{40,48},{48,56},{56,64},{64,7... | collective-permute-start | bytes 215048 | tf_op jit(solution)/shard_map/ppermute | solution.py:43
  44.9 2.5 collective-permute-start.2
  47.9 1.4 copy.90
  49.3 1.3 collective-permute-start.3
  50.6 0.8 copy.88
  51.4 3.0 %collective-permute-start = (f32[35,4,16,1]{0,2,3,1:T(8,128)S(1)}, f32[35,4,16,1]{0,2,3,1:T(8,128)S(1)}, u32[]{:S(2)}, u32[]{:S(2)}) collective-permute-start(f32[35,4,16,1]{0,2,3,1:T(8,128)S(1)} %copy.88), channel_id=1, source_target_pairs={{0,1},{1,2},{2,3},{3,4},{4,5},{5,6},{6,7},{8,9},{9,10},{10,11},{11... | collective-permute-start | bytes 26888 | tf_op jit(solution)/shard_map/ppermute | solution.py:43
  54.4 0.8 maximum_bitcast_fusion.1
  55.2 1.0 multiply_add_fusion
  56.2 2.0 copy.89
  58.2 1.5 pad.9
  59.8 2.0 copy.91
  61.8 1.5 pad.10
  63.4 0.9 maximum_bitcast_fusion
  64.5 4.1 %maximum_maximum_fusion = (f32[35,4,18,129]{3,2,1,0:T(8,128)S(1)}, f32[35,4,18,129]{3,2,1,0:T(8,128)S(1)}) fusion(f32[35,4,1,128]{3,2,1,0:T(1,128)} %collective-permute-done.2, f32[1,4,16,128]{3,2,1,0:T(8,128)S(1)} %get-tuple-element.260, f32[2,4,16,128]{3,2,1,0:T(8,128)S(1)} %slice.229, f32[32,4,16,128]{3,2,1,0:T(8,128)S(1)} %copy-done, ...), kind=kLoop, calls=%fused_computation.21 | loop fusion | flops 3250800 | bytes 3911040 | tf_op jit(solution)/shard_map/concatenate | solution.py:50
  69.3 1.3 maximum_maximum_fusion.1
  70.9 0.8 copy-done.8
  72.3 1.6 copy.93
  73.9 21.2 %all-to-all-start = ((f32[64,32,1,1,1,128]{5,1,4,3,2,0:T(8,128)}), f32[64,32,1,1,1,128]{5,1,4,3,2,0:T(8,128)S(1)}, u32[]{:S(2)}, u32[]{:S(2)}) async-start(f32[64,32,1,1,1,128]{5,1,4,3,2,0:T(8,128)} %copy.93), calls=%async_computation | async-start | bytes 2097152 | tf_op jit(solution)/shard_map/all_to_all | solution.py:30
  95.4 5.0 %sort.34 = (s32[2048]{0:T(1024)}, s32[2048]{0:T(1024)S(1)}) sort(s32[2048]{0:T(1024)S(1)} %neg.8, s32[2048]{0:T(1024)S(1)} %iota.8), dimensions={0}, to_apply=%region_0.1 | sort | flops 22528 | bytes 32768 | tf_op jit(solution)/shard_map/jit(argsort)/sort | solution.py:134
  100.5 5.0 %sort.35 = (s32[2048]{0:T(1024)}, s32[2048]{0:T(1024)S(1)}) sort(s32[2048]{0:T(1024)S(1)} %get-tuple-element.201, s32[2048]{0:T(1024)S(1)} %iota.9), dimensions={0}, to_apply=%region_6.9 | sort | flops 22528 | bytes 32768 | tf_op jit(solution)/shard_map/jit(argsort)/sort | solution.py:135
  105.5 11.8 %gather_fusion = s32[2048]{0:T(1024)S(1)} fusion(s32[2048]{0:T(1024)S(1)} %convert_element_type.20, s32[2048]{0:T(1024)S(1)} %get-tuple-element.274), kind=kCustom, calls=%fused_computation.4 | custom fusion | bytes 24576 | tf_op jit(solution)/shard_map/jit(_take)/gather | solution.py:138
  117.3 11.8 %gather_fusion.2 = f32[2048]{0:T(1024)S(1)} fusion(f32[2048]{0:T(1024)S(1)} %squeeze.14, s32[2048]{0:T(1024)S(1)} %get-tuple-element.274), kind=kCustom, calls=%fused_computation.1.clone | custom fusion | bytes 24576 | tf_op jit(solution)/shard_map/jit(_take)/gather | solution.py:137
  129.1 18.6 %all-to-all-done = f32[64,32,1,1,1,128]{5,1,4,3,2,0:T(8,128)S(1)} async-done(((f32[64,32,1,1,1,128]{5,1,4,3,2,0:T(8,128)}), f32[64,32,1,1,1,128]{5,1,4,3,2,0:T(8,128)S(1)}, u32[]{:S(2)}, u32[]{:S(2)}) %all-to-all-start) | async-done | bytes 1048608 | tf_op jit(solution)/shard_map/all_to_all | solution.py:30
  148.2 5.5 %gather_fusion.1 = f32[2048,128]{1,0:T(8,128)S(1)} fusion(f32[128,2048]{0,1:T(8,128)S(1)} %bitcast.130, s32[2048]{0:T(1024)S(1)} %get-tuple-element.274), kind=kCustom, calls=%fused_computation.clone | custom fusion | bytes 2105344 | tf_op jit(solution)/shard_map/jit(_take)/gather | solution.py:136
  153.7 1.3 select_bitcast_fusion.1
  155.0 1.0 broadcast_in_dim.65
  156.1 23.4 %while.38 = (s32[]{:T(128)}, f32[128,2048]{0,1:T(8,128)}, f32[2048]{0:T(1024)S(1)}, f32[128,2048]{0,1:T(8,128)}, s32[2048]{0:T(1024)S(1)}, /*index=5*/f32[2048]{...) while((s32[]{:T(128)}, f32[128,2048]{0,1:T(8,128)}, ...), condition=%wide.region_5.8_spmd, body=%wide.region_1.7_spmd.sunk | while | flops 135988224 | bytes 6311812 | solution.py:158
  156.2 0.7 fusion.68
  156.9 1.0 constant_dynamic-slice_fusion.2
  157.9 4.0 %while.39 = (s32[]{:T(128)}, f32[128,512]{0,1:T(8,128)S(1)}, s32[]{:T(128)}, s32[512]{0:T(512)S(1)}, f32[512]{0:T(512)S(1)}, /*index=5*/bf16[512,128]{1,0:T(8,128)(2,1)S(1)}, bf16[128,512]{1,0:T(8,128)(2,1)S(1)}, s32[]{:T(128)}) while((s32[]{:T(128)}, f32[128,512]{0,1:T(8,128)S(1)}, s32[]{:T(128)}, s32[512]{0:T(512)S(1)}, f32[512]{0:T(512)S(1)}, ...), condition=%wide.region_4.6_spmd, body=%wide.region_3.5_spmd.sunk | while | flops 135135744 | bytes 4199521 | solution.py:125
  158.8 0.7 fusion.73
  160.5 0.7 fusion.73
  162.5 0.7 constant_dynamic-update-slice_fusion.7
  163.3 0.7 fusion.68
  164.0 1.0 constant_dynamic-slice_fusion.2
  165.0 2.3 while.39
  166.0 0.7 fusion.73
  167.9 0.7 constant_dynamic-update-slice_fusion.7
  168.7 0.7 fusion.68
  169.4 1.0 constant_dynamic-slice_fusion.2
  170.4 2.3 while.39
  171.4 0.7 fusion.73
  173.4 0.7 constant_dynamic-update-slice_fusion.7
  174.2 0.7 fusion.68
  174.9 1.0 constant_dynamic-slice_fusion.2
  175.9 2.3 while.39
  176.8 0.7 fusion.73
  178.8 0.7 constant_dynamic-update-slice_fusion.7
  179.5 11.8 %gather_fusion.4 = f32[2048]{0:T(1024)S(1)} fusion(f32[2048]{0:T(1024)S(1)} %get-tuple-element.480, s32[2048]{0:T(1024)S(1)} %get-tuple-element.275), kind=kCustom, calls=%fused_computation.3.clone | custom fusion | bytes 24576 | tf_op jit(solution)/shard_map/jit(_take)/gather | solution.py:164
  191.3 5.5 %gather_fusion.3 = f32[2048,128]{1,0:T(8,128)S(1)} fusion(f32[128,2048]{0,1:T(8,128)S(1)} %copy-done.1, s32[2048]{0:T(1024)S(1)} %get-tuple-element.275), kind=kCustom, calls=%fused_computation.2.clone | custom fusion | bytes 2105344 | tf_op jit(solution)/shard_map/jit(_take)/gather | solution.py:164
  197.4 12.2 %all-to-all-start.3 = ((f32[64,1,1,1,1,128]{5,4,3,2,1,0:T(1,128)}), f32[64,1,1,1,1,128]{5,4,3,2,1,0:T(1,128)S(1)}, u32[]{:S(2)}, u32[]{:S(2)}) async-start(f32[64,1,1,1,1,128]{5,4,3,2,1,0:T(1,128)} %bitcast.45), calls=%async_computation.3 | async-start | bytes 65536 | tf_op jit(solution)/shard_map/all_to_all | solution.py:30
  210.4 1.3 copy.98
  211.7 13.6 %all-to-all-done.3 = f32[64,1,1,1,1,128]{5,4,3,2,1,0:T(1,128)S(1)} async-done(((f32[64,1,1,1,1,128]{5,4,3,2,1,0:T(1,128)}), f32[64,1,1,1,1,128]{5,4,3,2,1,0:T(1,128)S(1)}, u32[]{:S(2)}, u32[]{:S(2)}) %all-to-all-start.3) | async-done | bytes 32800 | tf_op jit(solution)/shard_map/all_to_all | solution.py:30
  225.4 6.3 %all-to-all-start.2 = ((f32[64,32,1,1,1,128]{5,1,4,3,2,0:T(8,128)}), f32[64,32,1,1,1,128]{5,1,4,3,2,0:T(8,128)}, u32[]{:S(2)}, u32[]{:S(2)}) async-start(f32[64,32,1,1,1,128]{5,1,4,3,2,0:T(8,128)} %bitcast.133), calls=%async_computation.2 | async-start | bytes 2097152 | tf_op jit(solution)/shard_map/all_to_all | solution.py:30
  231.8 1.2 fusion.20
  233.3 1.3 fusion.47
  234.7 1.3 dynamic-slice_add_fusion
  236.0 47.2 %all-to-all-done.2 = f32[64,32,1,1,1,128]{5,1,4,3,2,0:T(8,128)} async-done(((f32[64,32,1,1,1,128]{5,1,4,3,2,0:T(8,128)}), f32[64,32,1,1,1,128]{5,1,4,3,2,0:T(8,128)}, u32[]{:S(2)}, u32[]{:S(2)}) %all-to-all-start.2) | async-done | bytes 1048608 | tf_op jit(solution)/shard_map/all_to_all | solution.py:30
  283.2 2.8 copy.106
  (101 shorter events, 13.3 us)
Async XLA Ops:
  0.6 46.8 %copy-start = (f32[32,4,16,128]{3,2,1,0:T(8,128)S(1)}, f32[32,4,16,128]{3,2,1,0:T(8,128)}, u32[]{:S(2)}) copy-start(f32[32,4,16,128]{3,2,1,0:T(8,128)} %param.18) | copy-start | bytes 3145732
  16.8 30.6 %copy-start.9 = (f32[5,4,16,128]{3,2,1,0:T(8,128)}, f32[5,4,16,128]{3,2,1,0:T(8,128)S(1)}, u32[]{:S(2)}) copy-start(f32[5,4,16,128]{3,2,1,0:T(8,128)S(1)} %all_gather.3) | copy-start | bytes 491524
  19.0 54.9 %all-to-all-start.1 = ((f32[64,1,1,1,1,64]{5,4,3,2,1,0:T(1,128)}), f32[64,1,1,1,1,64]{5,4,3,2,1,0:T(1,128)S(1)}, u32[]{:S(2)}, u32[]{:S(2)}) async-start(f32[64,1,1,1,1,64]{5,4,3,2,1,0:T(1,128)} %bitcast.11), calls=%async_computation.1 | async-start | bytes 65536 | tf_op jit(solution)/shard_map/all_to_all | solution.py:30
  41.6 21.8 %collective-permute-start.1 = (f32[35,4,1,128]{3,2,1,0:T(1,128)}, f32[35,4,1,128]{3,2,1,0:T(1,128)S(1)}, u32[]{:S(2)}, u32[]{:S(2)}) collective-permute-start(f32[35,4,1,128]{3,2,1,0:T(1,128)} %get-tuple-element.257), channel_id=1, source_target_pairs={{0,8},{8,16},{16,24},{24,32},{32,40},{40,48},{48,56},{56,64},{64,7... | collective-permute-start | bytes 215048 | tf_op jit(solution)/shard_map/ppermute | solution.py:43
  44.9 18.4 %collective-permute-start.2 = (f32[35,4,1,128]{3,2,1,0:T(1,128)}, f32[35,4,1,128]{3,2,1,0:T(1,128)}, u32[]{:S(2)}, u32[]{:S(2)}) collective-permute-start(f32[35,4,1,128]{3,2,1,0:T(1,128)} %get-tuple-element.258), channel_id=1, source_target_pairs={{8,0},{16,8},{24,16},{32,24},{40,32},{48,40},{56,48},{64,56},{72,6... | collective-permute-start | bytes 215048 | tf_op jit(solution)/shard_map/ppermute | solution.py:44
  49.3 10.5 %collective-permute-start.3 = (f32[35,4,16,1]{0,2,3,1:T(8,128)}, f32[35,4,16,1]{0,2,3,1:T(8,128)S(1)}, u32[]{:S(2)}, u32[]{:S(2)}) collective-permute-start(f32[35,4,16,1]{0,2,3,1:T(8,128)} %copy.90), channel_id=1, source_target_pairs={{1,0},{2,1},{3,2},{4,3},{5,4},{6,5},{7,6},{9,8},{10,9},{11,10},{12... | collective-permute-start | bytes 26888 | tf_op jit(solution)/shard_map/ppermute | solution.py:44
  51.4 4.8 %collective-permute-start = (f32[35,4,16,1]{0,2,3,1:T(8,128)S(1)}, f32[35,4,16,1]{0,2,3,1:T(8,128)S(1)}, u32[]{:S(2)}, u32[]{:S(2)}) collective-permute-start(f32[35,4,16,1]{0,2,3,1:T(8,128)S(1)} %copy.88), channel_id=1, source_target_pairs={{0,1},{1,2},{2,3},{3,4},{4,5},{5,6},{6,7},{8,9},{9,10},{10,11},{11... | collective-permute-start | bytes 26888 | tf_op jit(solution)/shard_map/ppermute | solution.py:43
  59.8 4.7 %copy-start.4 = (f32[35,4,18,1]{3,2,1,0:T(8,128)}, f32[35,4,18,1]{3,2,1,0:T(8,128)S(1)}, u32[]{:S(2)}) copy-start(f32[35,4,18,1]{3,2,1,0:T(8,128)S(1)} %pad.9) | copy-start | bytes 30244
  63.3 1.2 copy-start.6
  70.6 1.1 copy-start.8
  73.9 73.8 %all-to-all-start = ((f32[64,32,1,1,1,128]{5,1,4,3,2,0:T(8,128)}), f32[64,32,1,1,1,128]{5,1,4,3,2,0:T(8,128)S(1)}, u32[]{:S(2)}, u32[]{:S(2)}) async-start(f32[64,32,1,1,1,128]{5,1,4,3,2,0:T(8,128)} %copy.93), calls=%async_computation | async-start | bytes 2097152 | tf_op jit(solution)/shard_map/all_to_all | solution.py:30
  153.6 2.4 copy-start.2
  153.6 2.4 copy-start.3
  153.7 2.4 copy-start.10
  179.5 11.8 %copy-start.1 = (f32[128,2048]{0,1:T(8,128)S(1)}, f32[128,2048]{0,1:T(8,128)}, u32[]{:S(2)}) copy-start(f32[128,2048]{0,1:T(8,128)} %get-tuple-element.479) | copy-start | bytes 3145732
  197.4 28.0 %all-to-all-start.3 = ((f32[64,1,1,1,1,128]{5,4,3,2,1,0:T(1,128)}), f32[64,1,1,1,1,128]{5,4,3,2,1,0:T(1,128)S(1)}, u32[]{:S(2)}, u32[]{:S(2)}) async-start(f32[64,1,1,1,1,128]{5,4,3,2,1,0:T(1,128)} %bitcast.45), calls=%async_computation.3 | async-start | bytes 65536 | tf_op jit(solution)/shard_map/all_to_all | solution.py:30
  211.7 20.0 %copy-start.5 = (f32[35,4,18,1]{3,2,1,0:T(8,128)S(1)}, f32[35,4,18,1]{3,2,1,0:T(8,128)}, u32[]{:S(2)}) copy-start(f32[35,4,18,1]{3,2,1,0:T(8,128)} %copy-done.4) | copy-start | bytes 30244
  225.4 57.8 %all-to-all-start.2 = ((f32[64,32,1,1,1,128]{5,1,4,3,2,0:T(8,128)}), f32[64,32,1,1,1,128]{5,1,4,3,2,0:T(8,128)}, u32[]{:S(2)}, u32[]{:S(2)}) async-start(f32[64,32,1,1,1,128]{5,1,4,3,2,0:T(8,128)} %bitcast.133), calls=%async_computation.2 | async-start | bytes 2097152 | tf_op jit(solution)/shard_map/all_to_all | solution.py:30
  231.8 1.6 copy-start.7
where the time goes:
time: 287 us; the launch traced here: 286 us
  local copies, waits for them, and re-layouts  79.4 us (28%)
  waiting for transfers between devices  79.4 us (28%)
  starting transfers between devices  70.3 us (24%)
  other arithmetic  32 us (11%)
  blocking collectives  12.6 us (4%)
  loops' own time  6.19 us (2%)
  matrix products  4.96 us (2%)
    all_to_all x4, waiting for transfers between devices, one_exchange(): lax.all_to_all(pieces, axis, split_axis=0, concat_axis=0, tiled=True)  79.4 us
    all_to_all x4, starting transfers between devices, one_exchange(): lax.all_to_all(pieces, axis, split_axis=0, concat_axis=0, tiled=True)  60.2 us
    gather x2, local copies, waits for them, and re-layouts, react_cells(): return (jnp.take(reacted, inverse, axis=1), jnp.take(heated, inverse))  17.2 us
    all_gather x1, blocking collectives, local(): lax.all_gather(jnp.stack([zonal_cell_fraction, meridional_cell_fraction,...  12.6 us
    gather x1, local copies, waits for them, and re-layouts, react_cells(): sorted_rates = jnp.take(rate_cells, sort_order)  11.8 us
    gather x1, local copies, waits for them, and re-layouts, react_cells(): sorted_counts = jnp.take(count_cells, sort_order)  11.8 us
    ppermute x2, starting transfers between devices, extended(): lax.ppermute(last, axis, up)  6.38 us
    another operation x4, loops' own time, react_block(): lax.while_loop(keep_going, substep, (jnp.zeros((), jnp.int32), tracer_blo...  6.09 us
  transfers between devices with their start and end apart: 8, of which 3 were waited for; matrix products, arithmetic and copies ran while one was open for 22% of the time, Pallas kernels for 0%

commit v1 on v0

--- a/solution.py
+++ b/solution.py
@@ -226,20 +226,17 @@
     own_group = lax.axis_index("group")
     local_strata = warmth_anomaly.shape[0]
     owned_tracers = species_amounts.shape[0]
-    columns = lax.all_gather(
-        jnp.stack(
-            [
-                zonal_cell_fraction,
-                meridional_cell_fraction,
-                updraft_cell_fraction,
-                warmth_anomaly,
-                mass_per_volume,
-            ]
-        ),
-        "group",
-        axis=1,
-        tiled=True,
-    )
+    x = jnp.stack(
+        [
+            zonal_cell_fraction,
+            meridional_cell_fraction,
+            updraft_cell_fraction,
+            warmth_anomaly,
+            mass_per_volume,
+        ]
+    )
+    outgoing = jnp.stack([x] * lax.axis_size("group"))
+    columns = jnp.concatenate(lax.all_to_all(outgoing, "group", 0, 0), axis=1)
     zonal_axis_name, meridional_axis_name, upward, heat_snapshot, air_density = (
         columns[0],
         columns[1],

time: 287 us -> 293 us (1.021)
  the two profiles are of different devices: /device:TPU:2 before, /device:TPU:32 now
where the time goes in v1:
time: 293 us; the launch traced here: 292 us
  waiting for transfers between devices  93.9 us (32%)
  local copies, waits for them, and re-layouts  82.6 us (28%)
  starting transfers between devices  65.9 us (22%)
  other arithmetic  36.9 us (13%)
  loops' own time  6.19 us (2%)
  matrix products  4.96 us (2%)
    all_to_all x4, waiting for transfers between devices, one_exchange(): lax.all_to_all(pieces, axis, split_axis=0, concat_axis=0, tiled=True)  85.8 us
    all_to_all x4, starting transfers between devices, one_exchange(): lax.all_to_all(pieces, axis, split_axis=0, concat_axis=0, tiled=True)  51.8 us
    gather x2, local copies, waits for them, and re-layouts, react_cells(): return (jnp.take(reacted, inverse, axis=1), jnp.take(heated, inverse))  17.2 us
    gather x1, local copies, waits for them, and re-layouts, react_cells(): sorted_rates = jnp.take(rate_cells, sort_order)  11.8 us
    gather x1, local copies, waits for them, and re-layouts, react_cells(): sorted_counts = jnp.take(count_cells, sort_order)  11.8 us
    concatenate x3, other arithmetic, extended(): jnp.concatenate([jnp.pad(low, around), value, jnp.pad(high, around)], axi...  10.7 us
    ppermute x2, starting transfers between devices, extended(): lax.ppermute(last, axis, up)  6.43 us
    another operation x4, loops' own time, react_block(): lax.while_loop(keep_going, substep, (jnp.zeros((), jnp.int32), tracer_blo...  6.09 us
  transfers between devices with their start and end apart: 9, of which 5 were waited for; matrix products, arithmetic and copies ran while one was open for 24% of the time, Pallas kernels for 0%

profile of v1, /device:TPU:32, one launch (start us, length us, event | category | flops | bytes accessed | tf_op | source)
XLA Modules:
  0.0 291.7 jit_solution(2447365810936025451)
XLA Ops:
  0.6 0.8 constant_dynamic-update-slice_fusion.5
  4.9 4.5 %all-to-all-start = ((f32[4,5,1,16,128]{4,3,2,1,0:T(8,128)}), f32[4,5,1,16,128]{4,3,2,1,0:T(8,128)S(1)}, u32[]{:S(2)}, u32[]{:S(2)}) async-start(f32[4,5,1,16,128]{4,3,2,1,0:T(8,128)} %stack.34), calls=%async_computation | async-start | bytes 327680 | tf_op jit(solution)/shard_map/all_to_all | solution.py:239
  9.4 0.8 dynamic-slice_convert_fusion
  10.1 5.4 %all-to-all-done = f32[4,5,1,16,128]{4,3,2,1,0:T(8,128)S(1)} async-done(((f32[4,5,1,16,128]{4,3,2,1,0:T(8,128)}), f32[4,5,1,16,128]{4,3,2,1,0:T(8,128)S(1)}, u32[]{:S(2)}, u32[]{:S(2)}) %all-to-all-start) | async-done | bytes 163872 | tf_op jit(solution)/shard_map/all_to_all | solution.py:239
  16.8 2.0 pad_maximum_fusion.6
  19.7 18.5 %all-to-all-start.2 = ((f32[64,1,1,1,1,64]{5,4,3,2,1,0:T(1,128)}), f32[64,1,1,1,1,64]{5,4,3,2,1,0:T(1,128)}, u32[]{:S(2)}, u32[]{:S(2)}) async-start(f32[64,1,1,1,1,64]{5,4,3,2,1,0:T(1,128)} %bitcast.12), calls=%async_computation.2 | async-start | bytes 65536 | tf_op jit(solution)/shard_map/all_to_all | solution.py:30
  38.2 4.0 %collective-permute-start.1 = (f32[35,4,1,128]{3,2,1,0:T(1,128)}, f32[35,4,1,128]{3,2,1,0:T(1,128)}, u32[]{:S(2)}, u32[]{:S(2)}) collective-permute-start(f32[35,4,1,128]{3,2,1,0:T(1,128)} %get-tuple-element.253), channel_id=1, source_target_pairs={{0,8},{8,16},{16,24},{24,32},{32,40},{40,48},{48,56},{56,64},{64,7... | collective-permute-start | bytes 215048 | tf_op jit(solution)/shard_map/ppermute | solution.py:43
  42.2 1.3 collective-permute-start.2
  43.5 1.4 fusion.55
  45.0 1.9 copy.53
  46.9 1.4 copy.55
  48.3 1.9 collective-permute-start.3
  50.2 2.4 collective-permute-start
  52.8 2.7 collective-permute-done
  55.5 2.0 copy.54
  57.5 1.5 pad.9
  59.0 2.8 copy.56
  61.8 1.5 pad.10
  63.4 4.8 %pad_maximum_fusion = f32[35,4,18,130]{3,2,1,0:T(8,128)S(1)} fusion(f32[35,4,18,1]{3,2,1,0:T(8,128)S(1)} %pad.10, f32[35,4,1,128]{3,2,1,0:T(1,128)} %collective-permute-done.2, f32[1,4,16,128]{3,2,1,0:T(8,128)S(1)} %copy-done.12, f32[1,4,16,128]{3,2,1,0:T(8,128)S(1)} %copy-done.15, f32[1,4,16,128]{3,2,1,0:T(8,128)S(1)} %copy-done.9, ...), kind=kLoop, calls=%fused_computation.21 | loop fusion | flops 2293200 | bytes 2620800 | tf_op jit(solution)/shard_map/concatenate | solution.py:50
  68.5 4.6 %maximum_maximum_fusion = (f32[35,4,18,129]{3,2,1,0:T(8,128)S(1)}, f32[35,4,18,129]{3,2,1,0:T(8,128)S(1)}) fusion(f32[35,4,1,128]{3,2,1,0:T(1,128)} %collective-permute-done.2, f32[1,4,16,128]{3,2,1,0:T(8,128)S(1)} %copy-done.12, f32[1,4,16,128]{3,2,1,0:T(8,128)S(1)} %copy-done.15, f32[1,4,16,128]{3,2,1,0:T(8,128)S(1)} %copy-done.9, ...), kind=kLoop, calls=%fused_computation.22 | loop fusion | flops 3900960 | bytes 3911040 | tf_op jit(solution)/shard_map/concatenate | solution.py:50
  73.7 1.4 maximum_maximum_fusion.1
  76.1 1.6 copy.57
  77.7 21.8 %all-to-all-start.1 = ((f32[64,32,1,1,1,128]{5,1,4,3,2,0:T(8,128)}), f32[64,32,1,1,1,128]{5,1,4,3,2,0:T(8,128)S(1)}, u32[]{:S(2)}, u32[]{:S(2)}) async-start(f32[64,32,1,1,1,128]{5,1,4,3,2,0:T(8,128)} %copy.57), calls=%async_computation.1 | async-start | bytes 2097152 | tf_op jit(solution)/shard_map/all_to_all | solution.py:30
  99.5 0.9 reshape_reshape.7
  100.6 5.0 %sort.34 = (s32[2048]{0:T(1024)}, s32[2048]{0:T(1024)S(1)}) sort(s32[2048]{0:T(1024)S(1)} %neg.8, s32[2048]{0:T(1024)S(1)} %iota.8), dimensions={0}, to_apply=%region_0.1 | sort | flops 22528 | bytes 32768 | tf_op jit(solution)/shard_map/jit(argsort)/sort | solution.py:134
  105.6 5.0 %sort.35 = (s32[2048]{0:T(1024)}, s32[2048]{0:T(1024)S(1)}) sort(s32[2048]{0:T(1024)S(1)} %get-tuple-element.201, s32[2048]{0:T(1024)S(1)} %iota.9), dimensions={0}, to_apply=%region_6.9 | sort | flops 22528 | bytes 32768 | tf_op jit(solution)/shard_map/jit(argsort)/sort | solution.py:135
  110.7 11.8 %gather_fusion = s32[2048]{0:T(1024)S(1)} fusion(s32[2048]{0:T(1024)S(1)} %convert_element_type.20, s32[2048]{0:T(1024)S(1)} %get-tuple-element.271), kind=kCustom, calls=%fused_computation.4 | custom fusion | bytes 24576 | tf_op jit(solution)/shard_map/jit(_take)/gather | solution.py:138
  122.5 11.8 %gather_fusion.2 = f32[2048]{0:T(1024)S(1)} fusion(f32[2048]{0:T(1024)S(1)} %squeeze.14, s32[2048]{0:T(1024)S(1)} %get-tuple-element.271), kind=kCustom, calls=%fused_computation.1.clone | custom fusion | bytes 24576 | tf_op jit(solution)/shard_map/jit(_take)/gather | solution.py:137
  134.3 21.2 %all-to-all-done.1 = f32[64,32,1,1,1,128]{5,1,4,3,2,0:T(8,128)S(1)} async-done(((f32[64,32,1,1,1,128]{5,1,4,3,2,0:T(8,128)}), f32[64,32,1,1,1,128]{5,1,4,3,2,0:T(8,128)S(1)}, u32[]{:S(2)}, u32[]{:S(2)}) %all-to-all-start.1) | async-done | bytes 1048608 | tf_op jit(solution)/shard_map/all_to_all | solution.py:30
  155.9 5.5 %gather_fusion.1 = f32[2048,128]{1,0:T(8,128)S(1)} fusion(f32[128,2048]{0,1:T(8,128)S(1)} %bitcast.143, s32[2048]{0:T(1024)S(1)} %get-tuple-element.271), kind=kCustom, calls=%fused_computation.clone | custom fusion | bytes 2105344 | tf_op jit(solution)/shard_map/jit(_take)/gather | solution.py:136
  161.5 1.3 select_bitcast_fusion.1
  162.8 1.0 broadcast_in_dim.65
  163.8 23.4 %while.38 = (s32[]{:T(128)}, f32[128,2048]{0,1:T(8,128)}, f32[2048]{0:T(1024)S(1)}, f32[128,2048]{0,1:T(8,128)}, s32[2048]{0:T(1024)S(1)}, /*index=5*/f32[2048]{...) while((s32[]{:T(128)}, f32[128,2048]{0,1:T(8,128)}, ...), condition=%wide.region_5.8_spmd, body=%wide.region_1.7_spmd.sunk | while | flops 135988224 | bytes 6311812 | solution.py:158
  163.9 0.7 fusion.69
  164.6 1.0 constant_dynamic-slice_fusion.2
  165.6 4.0 %while.39 = (s32[]{:T(128)}, f32[128,512]{0,1:T(8,128)S(1)}, s32[]{:T(128)}, s32[512]{0:T(512)S(1)}, f32[512]{0:T(512)S(1)}, /*index=5*/bf16[512,128]{1,0:T(8,128)(2,1)S(1)}, bf16[128,512]{1,0:T(8,128)(2,1)S(1)}, s32[]{:T(128)}) while((s32[]{:T(128)}, f32[128,512]{0,1:T(8,128)S(1)}, s32[]{:T(128)}, s32[512]{0:T(512)S(1)}, f32[512]{0:T(512)S(1)}, ...), condition=%wide.region_4.6_spmd, body=%wide.region_3.5_spmd.sunk | while | flops 135135744 | bytes 4199521 | solution.py:125
  166.6 0.7 fusion.74
  168.3 0.7 fusion.74
  170.3 0.7 constant_dynamic-update-slice_fusion.7
  171.8 1.0 constant_dynamic-slice_fusion.2
  172.7 2.3 while.39
  173.7 0.7 fusion.74
  175.7 0.7 constant_dynamic-update-slice_fusion.7
  176.5 0.7 fusion.69
  177.2 1.0 constant_dynamic-slice_fusion.2
  178.2 2.3 while.39
  179.2 0.7 fusion.74
  181.1 0.7 constant_dynamic-update-slice_fusion.7
  182.6 1.0 constant_dynamic-slice_fusion.2
  183.6 2.3 while.39
  184.6 0.7 fusion.74
  186.5 0.7 constant_dynamic-update-slice_fusion.7
  187.3 11.8 %gather_fusion.4 = f32[2048]{0:T(1024)S(1)} fusion(f32[2048]{0:T(1024)S(1)} %get-tuple-element.477, s32[2048]{0:T(1024)S(1)} %get-tuple-element.272), kind=kCustom, calls=%fused_computation.3.clone | custom fusion | bytes 24576 | tf_op jit(solution)/shard_map/jit(_take)/gather | solution.py:164
  199.1 5.5 %gather_fusion.3 = f32[2048,128]{1,0:T(8,128)S(1)} fusion(f32[128,2048]{0,1:T(8,128)S(1)} %copy-done.1, s32[2048]{0:T(1024)S(1)} %get-tuple-element.272), kind=kCustom, calls=%fused_computation.2.clone | custom fusion | bytes 2105344 | tf_op jit(solution)/shard_map/jit(_take)/gather | solution.py:164
  205.1 6.0 %all-to-all-start.4 = ((f32[64,1,1,1,1,128]{5,4,3,2,1,0:T(1,128)}), f32[64,1,1,1,1,128]{5,4,3,2,1,0:T(1,128)S(1)}, u32[]{:S(2)}, u32[]{:S(2)}) async-start(f32[64,1,1,1,1,128]{5,4,3,2,1,0:T(1,128)} %bitcast.49), calls=%async_computation.4 | async-start | bytes 65536 | tf_op jit(solution)/shard_map/all_to_all | solution.py:30
  212.1 1.3 copy.62
  213.3 14.6 %all-to-all-done.4 = f32[64,1,1,1,1,128]{5,4,3,2,1,0:T(1,128)S(1)} async-done(((f32[64,1,1,1,1,128]{5,4,3,2,1,0:T(1,128)}), f32[64,1,1,1,1,128]{5,4,3,2,1,0:T(1,128)S(1)}, u32[]{:S(2)}, u32[]{:S(2)}) %all-to-all-start.4) | async-done | bytes 32800 | tf_op jit(solution)/shard_map/all_to_all | solution.py:30
  228.0 5.5 %all-to-all-start.3 = ((f32[64,32,1,1,1,128]{5,1,4,3,2,0:T(8,128)}), f32[64,32,1,1,1,128]{5,1,4,3,2,0:T(8,128)}, u32[]{:S(2)}, u32[]{:S(2)}) async-start(f32[64,32,1,1,1,128]{5,1,4,3,2,0:T(8,128)} %bitcast.146), calls=%async_computation.3 | async-start | bytes 2097152 | tf_op jit(solution)/shard_map/all_to_all | solution.py:30
  233.6 1.3 fusion.20
  234.9 1.3 fusion.47
  236.2 1.4 fusion.36
  237.6 1.3 dynamic-slice_add_fusion
  238.9 49.9 %all-to-all-done.3 = f32[64,32,1,1,1,128]{5,1,4,3,2,0:T(8,128)} async-done(((f32[64,32,1,1,1,128]{5,1,4,3,2,0:T(8,128)}), f32[64,32,1,1,1,128]{5,1,4,3,2,0:T(8,128)}, u32[]{:S(2)}, u32[]{:S(2)}) %all-to-all-start.3) | async-done | bytes 1048608 | tf_op jit(solution)/shard_map/all_to_all | solution.py:30
  288.9 2.8 copy.71
  (122 shorter events, 15.3 us)
Async XLA Ops:
  0.6 18.1 %copy-start = (f32[32,4,16,128]{3,2,1,0:T(8,128)S(1)}, f32[32,4,16,128]{3,2,1,0:T(8,128)}, u32[]{:S(2)}) copy-start(f32[32,4,16,128]{3,2,1,0:T(8,128)} %param.18) | copy-start | bytes 3145732
  4.9 10.6 %all-to-all-start = ((f32[4,5,1,16,128]{4,3,2,1,0:T(8,128)}), f32[4,5,1,16,128]{4,3,2,1,0:T(8,128)S(1)}, u32[]{:S(2)}, u32[]{:S(2)}) async-start(f32[4,5,1,16,128]{4,3,2,1,0:T(8,128)} %stack.34), calls=%async_computation | async-start | bytes 327680 | tf_op jit(solution)/shard_map/all_to_all | solution.py:239
  16.7 2.0 copy-start.8
  16.8 2.1 copy-start.11
  16.8 2.1 copy-start.14
  19.7 58.0 %all-to-all-start.2 = ((f32[64,1,1,1,1,64]{5,4,3,2,1,0:T(1,128)}), f32[64,1,1,1,1,64]{5,4,3,2,1,0:T(1,128)}, u32[]{:S(2)}, u32[]{:S(2)}) async-start(f32[64,1,1,1,1,64]{5,4,3,2,1,0:T(1,128)} %bitcast.12), calls=%async_computation.2 | async-start | bytes 65536 | tf_op jit(solution)/shard_map/all_to_all | solution.py:30
  38.2 25.2 %collective-permute-start.1 = (f32[35,4,1,128]{3,2,1,0:T(1,128)}, f32[35,4,1,128]{3,2,1,0:T(1,128)}, u32[]{:S(2)}, u32[]{:S(2)}) collective-permute-start(f32[35,4,1,128]{3,2,1,0:T(1,128)} %get-tuple-element.253), channel_id=1, source_target_pairs={{0,8},{8,16},{16,24},{24,32},{32,40},{40,48},{48,56},{56,64},{64,7... | collective-permute-start | bytes 215048 | tf_op jit(solution)/shard_map/ppermute | solution.py:43
  42.2 21.1 %collective-permute-start.2 = (f32[35,4,1,128]{3,2,1,0:T(1,128)}, f32[35,4,1,128]{3,2,1,0:T(1,128)}, u32[]{:S(2)}, u32[]{:S(2)}) collective-permute-start(f32[35,4,1,128]{3,2,1,0:T(1,128)} %get-tuple-element.254), channel_id=1, source_target_pairs={{8,0},{16,8},{24,16},{32,24},{40,32},{48,40},{56,48},{64,56},{72,6... | collective-permute-start | bytes 215048 | tf_op jit(solution)/shard_map/ppermute | solution.py:44
  45.0 7.7 %copy-start.17 = (f32[3,16,128]{2,1,0:T(8,128)S(1)}, f32[3,16,128]{2,1,0:T(8,128)}, u32[]{:S(2)}) copy-start(f32[3,16,128]{2,1,0:T(8,128)} %get-tuple-element.260) | copy-start | bytes 73732
  45.0 7.7 %copy-start.18 = (f32[3,16,128]{2,1,0:T(8,128)S(1)}, f32[3,16,128]{2,1,0:T(8,128)}, u32[]{:S(2)}) copy-start(f32[3,16,128]{2,1,0:T(8,128)} %get-tuple-element.261) | copy-start | bytes 73732
  48.3 10.7 %collective-permute-start.3 = (f32[35,4,16,1]{0,2,3,1:T(8,128)}, f32[35,4,16,1]{0,2,3,1:T(8,128)}, u32[]{:S(2)}, u32[]{:S(2)}) collective-permute-start(f32[35,4,16,1]{0,2,3,1:T(8,128)} %copy.55), channel_id=1, source_target_pairs={{1,0},{2,1},{3,2},{4,3},{5,4},{6,5},{7,6},{9,8},{10,9},{11,10},{12... | collective-permute-start | bytes 26888 | tf_op jit(solution)/shard_map/ppermute | solution.py:44
  50.2 5.2 %collective-permute-start = (f32[35,4,16,1]{0,2,3,1:T(8,128)S(1)}, f32[35,4,16,1]{0,2,3,1:T(8,128)S(1)}, u32[]{:S(2)}, u32[]{:S(2)}) collective-permute-start(f32[35,4,16,1]{0,2,3,1:T(8,128)S(1)} %copy.53), channel_id=1, source_target_pairs={{0,1},{1,2},{2,3},{3,4},{4,5},{5,6},{6,7},{8,9},{9,10},{10,11},{11... | collective-permute-start | bytes 26888 | tf_op jit(solution)/shard_map/ppermute | solution.py:43
  59.0 9.5 %copy-start.4 = (f32[35,4,18,1]{3,2,1,0:T(8,128)}, f32[35,4,18,1]{3,2,1,0:T(8,128)S(1)}, u32[]{:S(2)}) copy-start(f32[35,4,18,1]{3,2,1,0:T(8,128)S(1)} %pad.9) | copy-start | bytes 30244
  61.8 1.6 copy-start.9
  61.8 1.6 copy-start.12
  61.8 1.6 copy-start.15
  63.4 5.1 %copy-start.6 = (f32[35,4,18,1]{3,2,1,0:T(8,128)}, f32[35,4,18,1]{3,2,1,0:T(8,128)S(1)}, u32[]{:S(2)}) copy-start(f32[35,4,18,1]{3,2,1,0:T(8,128)S(1)} %pad.10) | copy-start | bytes 30244
  77.7 77.9 %all-to-all-start.1 = ((f32[64,32,1,1,1,128]{5,1,4,3,2,0:T(8,128)}), f32[64,32,1,1,1,128]{5,1,4,3,2,0:T(8,128)S(1)}, u32[]{:S(2)}, u32[]{:S(2)}) async-start(f32[64,32,1,1,1,128]{5,1,4,3,2,0:T(8,128)} %copy.57), calls=%async_computation.1 | async-start | bytes 2097152 | tf_op jit(solution)/shard_map/all_to_all | solution.py:30
  161.4 2.4 copy-start.2
  161.4 2.4 copy-start.3
  161.4 2.4 copy-start.19
  187.3 11.8 %copy-start.1 = (f32[128,2048]{0,1:T(8,128)S(1)}, f32[128,2048]{0,1:T(8,128)}, u32[]{:S(2)}) copy-start(f32[128,2048]{0,1:T(8,128)} %get-tuple-element.476) | copy-start | bytes 3145732
  205.1 22.8 %all-to-all-start.4 = ((f32[64,1,1,1,1,128]{5,4,3,2,1,0:T(1,128)}), f32[64,1,1,1,1,128]{5,4,3,2,1,0:T(1,128)S(1)}, u32[]{:S(2)}, u32[]{:S(2)}) async-start(f32[64,1,1,1,1,128]{5,4,3,2,1,0:T(1,128)} %bitcast.49), calls=%async_computation.4 | async-start | bytes 65536 | tf_op jit(solution)/shard_map/all_to_all | solution.py:30
  212.0 21.5 %copy-start.10 = (f32[1,4,16,128]{3,2,1,0:T(8,128)S(1)}, f32[1,4,16,128]{3,2,1,0:T(8,128)}, u32[]{:S(2)}) copy-start(f32[1,4,16,128]{3,2,1,0:T(8,128)} %copy-done.8) | copy-start | bytes 98308
  212.0 21.5 %copy-start.13 = (f32[1,4,16,128]{3,2,1,0:T(8,128)S(1)}, f32[1,4,16,128]{3,2,1,0:T(8,128)}, u32[]{:S(2)}) copy-start(f32[1,4,16,128]{3,2,1,0:T(8,128)} %copy-done.11) | copy-start | bytes 98308
  212.0 21.5 %copy-start.16 = (f32[1,4,16,128]{3,2,1,0:T(8,128)S(1)}, f32[1,4,16,128]{3,2,1,0:T(8,128)}, u32[]{:S(2)}) copy-start(f32[1,4,16,128]{3,2,1,0:T(8,128)} %copy-done.14) | copy-start | bytes 98308
  213.3 20.3 %copy-start.5 = (f32[35,4,18,1]{3,2,1,0:T(8,128)S(1)}, f32[35,4,18,1]{3,2,1,0:T(8,128)}, u32[]{:S(2)}) copy-start(f32[35,4,18,1]{3,2,1,0:T(8,128)} %copy-done.4) | copy-start | bytes 30244
  228.0 60.9 %all-to-all-start.3 = ((f32[64,32,1,1,1,128]{5,1,4,3,2,0:T(8,128)}), f32[64,32,1,1,1,128]{5,1,4,3,2,0:T(8,128)}, u32[]{:S(2)}, u32[]{:S(2)}) async-start(f32[64,32,1,1,1,128]{5,1,4,3,2,0:T(8,128)} %bitcast.146), calls=%async_computation.3 | async-start | bytes 2097152 | tf_op jit(solution)/shard_map/all_to_all | solution.py:30
  233.6 2.6 copy-start.7
